TPU v7x, 256 devices: a whole 4x4x8 slice. The times are simulated.
256 devices in a mesh: row: 8 (over y, core), col: 8 (over z), track: 4 (over x).
Axes of the slice: x: 4, y: 4, z: 8, core: 2. Of those that a mesh axis runs over, the one named last changes fastest.
Arguments:
- factors: float32 [16384, 2, 16, 576], P(('row', 'col', 'track')), may hold values from -0.5 to 0.5
- track_clusters: int32 [16384, 2], P(('row', 'col', 'track')), may hold values from 0 to 7, as said below
- filed_flip: int32 [16384], P(('row', 'col', 'track')), may hold values from 0 to 1, as said below
- damping: float32 [8, 576], P('row'), may hold values from 50 to 500
- rhs: float32 [8, 576], P('row'), may hold values from -3000 to 3000
Outputs:
- solution: float32 [8, 576], P('row')
- scaled_residual: float32 [8, 576], P('row')
- filed_blocks: float32 [8, 8, 576, 576], P('row', 'col', 'track')
Inputs may be any that keep to these rules, and one draw needn't show every extreme that they name: `track_clusters`: each row names two different clusters, the first below the second. `filed_flip`: the owner of a block filed under (i, j) is the device of row group i // 1 and column j, with the track index of the device that holds the track block. Of the 64 track blocks of one device at most 3 go to any one owner, and in every draw, for each track index, some owner receives exactly 3 from every device of that track index.
All inputs are finite; a program needn't handle non-finite values.
Results may differ from a plain program's by a relative error of at most 0.0003.
Values sent between devices are 32-bit elements; how exact they have to be, the bound alone decides.
No kernel may reach another device: no remote copies, remote signals or barrier semaphores. Data moves between devices by JAX's collectives and lax.ppermute only.
A program may use at most 128 MiB of HBM per device.

v0:
```python
import jax
import jax.numpy as jnp
from jax import lax
from jax.sharding import PartitionSpec as P

ITERS = 2
highest = lax.Precision.HIGHEST


def fitness_sum(residual, scaled):
    return lax.psum(jnp.sum(residual * scaled), "row")


def on_device(factors, track_clusters, filed_flip, damping, rhs):
    n_row = lax.axis_size("row")
    n_col = lax.axis_size("col")
    n_track = lax.axis_size("track")
    owners = n_row * n_col
    tb_dev = factors.shape[0]
    jac_rows = factors.shape[2]
    params = factors.shape[3]
    row_clusters = damping.shape[0]
    clusters = row_clusters * n_row
    capacity = 3 * tb_dev // owners
    row_share = params // n_track
    row_id = lax.axis_index("row")
    col_id = lax.axis_index("col")
    track_id = lax.axis_index("track")
    low_cluster = track_clusters[:, 0]
    high_cluster = track_clusters[:, 1]
    low_side = factors[:, 0]
    high_side = factors[:, 1]
    cluster_ids = jnp.arange(clusters, dtype=jnp.int32)
    low_onehot = (low_cluster[:, None] == cluster_ids[None, :]).astype(jnp.float32)
    high_onehot = (high_cluster[:, None] == cluster_ids[None, :]).astype(jnp.float32)
    diag_part = jnp.dot(low_onehot.T, jnp.sum(low_side * low_side, axis=1), precision=highest)
    diag_part = diag_part + jnp.dot(
        high_onehot.T, jnp.sum(high_side * high_side, axis=1), precision=highest
    )
    diag_all = lax.psum(diag_part, ("row", "col", "track"))
    precond = damping + lax.dynamic_slice_in_dim(diag_all, row_id * row_clusters, row_clusters, 0)
    flipped = filed_flip == 1
    filed_row = jnp.where(flipped, high_cluster, low_cluster)
    filed_col = jnp.where(flipped, low_cluster, high_cluster)
    oriented = jnp.where(flipped[:, None, None, None], factors[:, ::-1], factors)
    owner_row = filed_row // row_clusters
    target = owner_row * n_col + filed_col
    slot_ids = filed_row - owner_row * row_clusters
    owner_hits = (target[:, None] == jnp.arange(owners, dtype=jnp.int32)[None, :]).astype(jnp.int32)
    places = jnp.sum((jnp.cumsum(owner_hits, axis=0) - 1) * owner_hits, axis=1)
    position = target * capacity + places
    outgoing = (
        jnp.zeros((owners * capacity, 2, jac_rows, params), jnp.float32).at[position].set(oriented)
    )
    outgoing_slots = jnp.zeros((owners * capacity,), jnp.int32).at[position].set(slot_ids)
    incoming, incoming_slots = (
        lax.all_to_all(
            outgoing.reshape(owners, capacity, 2, jac_rows, params),
            ("row", "col"),
            split_axis=0,
            concat_axis=0,
            tiled=True,
        ),
        lax.all_to_all(
            outgoing_slots.reshape(owners, capacity),
            ("row", "col"),
            split_axis=0,
            concat_axis=0,
            tiled=True,
        ),
    )
    received = incoming.reshape(owners * capacity, 2, jac_rows, params)
    received_slots = incoming_slots.reshape(owners * capacity)
    received_rows = received[:, 0]
    received_cols = received[:, 1]
    slot_masks = [(received_slots == 0).astype(jnp.float32)]
    pieces = [
        jnp.einsum(
            "mkr,mkc->rc",
            received_rows * slot_mask[:, None, None],
            received_cols,
            precision=highest,
            preferred_element_type=jnp.float32,
        )
        for slot_mask in slot_masks
    ]
    filed = lax.psum_scatter(pieces[0], "track", scatter_dimension=0, tiled=True)
    filed_blocks = filed.reshape(row_share, row_clusters, params)
    blocks_out = jnp.transpose(filed_blocks, (1, 0, 2))[:, None]
    col_onehot = (cluster_ids == col_id).astype(jnp.float32)
    solution = jnp.zeros_like(rhs)
    residual = rhs
    scaled = residual / precond
    direction = scaled
    fitness = fitness_sum(residual, scaled)
    for iteration in range(ITERS):
        full_dir = lax.all_gather(direction, "row", axis=0, tiled=True)
        col_dir = jnp.dot(col_onehot, full_dir, precision=highest)
        own_share = lax.dynamic_slice_in_dim(direction, track_id * row_share, row_share, 1)
        row_terms = jnp.einsum("rsc,c->sr", filed_blocks, col_dir, precision=highest)
        col_terms = jnp.einsum("rsc,sr->c", filed_blocks, own_share, precision=highest)
        low_dir = jnp.dot(low_onehot, full_dir, precision=highest)
        high_dir = jnp.dot(high_onehot, full_dir, precision=highest)
        low_proj = jnp.einsum("mkc,mc->mk", low_side, low_dir, precision=highest)
        high_proj = jnp.einsum("mkc,mc->mk", high_side, high_dir, precision=highest)
        low_back = jnp.einsum("mk,mkc->mc", low_proj, low_side, precision=highest)
        high_back = jnp.einsum("mk,mkc->mc", high_proj, high_side, precision=highest)
        local = jnp.dot(low_onehot.T, low_back, precision=highest) + jnp.dot(
            high_onehot.T, high_back, precision=highest
        )
        placed = lax.dynamic_update_slice(
            jnp.zeros((clusters, params), jnp.float32),
            row_terms,
            (row_id * row_clusters, track_id * row_share),
        )
        local = local + placed + col_onehot[:, None] * col_terms[None, :]
        summed = lax.psum(local, ("row", "col", "track"))
        images = (
            lax.dynamic_slice_in_dim(summed, row_id * row_clusters, row_clusters, 0)
            + damping * direction
        )
        curvature = lax.psum(jnp.sum(direction * images), "row")
        images, curvature = (images, curvature)
        step_size = fitness / curvature
        solution = solution + step_size * direction
        residual = residual - step_size * images
        scaled = residual / precond
        fitness_next = fitness_sum(residual, scaled)
        direction = scaled + fitness_next / fitness * direction
        fitness = fitness_next
    return (solution, scaled, blocks_out)


def solution(mesh):
    in_specs = (
        P(("row", "col", "track"), None, None, None),
        P(("row", "col", "track"), None),
        P(("row", "col", "track")),
        P("row", None),
        P("row", None),
    )
    out_specs = (P("row", None), P("row", None), P("row", "col", "track", None))
    return jax.shard_map(
        on_device, mesh=mesh, in_specs=in_specs, out_specs=out_specs, check_vma=False
    )
```

profile of v0, /device:TPU:1, one launch (start us, length us, event | category | flops | bytes accessed | tf_op | source)
XLA Modules:
  0.0 1023.1 jit_solution(7229425490721513363)
XLA Ops:
  7.2 0.8 select_add_fusion
  7.9 0.1 fusion.59
  8.0 0.1 reduce_window_sum.11
  8.1 0.2 select_reduce_fusion
  8.3 0.8 scatter_custom_fusion.1
  9.1 0.8 all_to_all.10
  9.8 13.1 %all-to-all-start.1 = ((s32[64,1,3]{2,1,0:T(1,128)}), s32[64,1,3]{2,1,0:T(1,128)S(1)}, u32[]{:S(2)}, u32[]{:S(2)}) async-start(s32[64,1,3]{2,1,0:T(1,128)} %bitcast.21), calls=%async_computation.1 | async-start | bytes 65536 | tf_op jit(solution)/shard_map/all_to_all | solution.py:64
  23.0 0.7 broadcast_compare_fusion
  23.7 6.9 reverse_select_fusion
  30.5 7.5 broadcast_in_dim.12
  38.0 13.0 %scatter_fusion = f32[192,2,16,576]{3,2,1,0:T(8,128)} fusion(f32[192,2,16,576]{3,2,1,0:T(8,128)} %broadcast_in_dim.12, s32[64]{0:T(128)S(1)} %compare_select_fusion, f32[64,2,16,576]{3,2,1,0:T(8,128)} %reverse_select_fusion), kind=kCustom, calls=%fused_computation | custom fusion | bytes 14156032 | tf_op jit(solution)/shard_map/scatter | solution.py:53
  51.1 10.7 %all-to-all-start = ((f32[64,3,2,16,576]{4,3,2,1,0:T(8,128)}), f32[64,3,2,16,576]{4,3,2,1,0:T(8,128)}, u32[]{:S(2)}, u32[]{:S(2)}) async-start(f32[64,3,2,16,576]{4,3,2,1,0:T(8,128)} %bitcast.149), calls=%async_computation | async-start | bytes 31457280 | tf_op jit(solution)/shard_map/all_to_all | solution.py:57
  61.8 0.0 reduce-scatter.2.cloned.1.call-start
  61.9 3.6 fusion.11
  65.4 0.3 fusion.60
  65.7 0.1 fusion.58
  65.8 0.1 reshape.60
  66.0 344.5 %all-to-all-done = f32[64,3,2,16,576]{4,3,2,1,0:T(8,128)} async-done(((f32[64,3,2,16,576]{4,3,2,1,0:T(8,128)}), f32[64,3,2,16,576]{4,3,2,1,0:T(8,128)}, u32[]{:S(2)}, u32[]{:S(2)}) %all-to-all-start) | async-done | bytes 14155808 | tf_op jit(solution)/shard_map/all_to_all | solution.py:57
  410.5 3.8 slice.25
  414.2 3.8 fusion
  418.1 0.0 copy-start.1
  418.1 0.0 copy-start.2
  418.1 247.6 %fusion.29 = f32[576,576]{1,0:T(8,128)} fusion(f32[192,1,16,576]{3,2,1,0:T(8,128)S(1)} %slice.25, f32[192,16,576]{2,1,0:T(8,128)S(1)} %fusion), kind=kOutput, calls=%fused_computation.36 | convolution fusion | flops 12230590464 | bytes 15482880 | tf_op jit(solution)/shard_map/mkr,mkc->rc/dot_general | solution.py:78
  665.7 0.0 reduce-scatter.2.cloned.1.call-update
  665.7 0.3 convolution_add_fusion.2
  666.0 89.9 %psum.49 = f32[8,576]{1,0:T(8,128)S(1)} all-reduce(f32[8,576]{1,0:T(8,128)S(1)} %convolution_add_fusion.2), channel_id=1, replica_groups=mesh['row'=8,'col'=8,'track'=4] {'row','col','track'}, use_global_device_ids=true, to_apply=%region_2.0 | all-reduce | flops 4608 | bytes 36864 | tf_op jit(solution)/shard_map/psum | solution.py:40
  755.9 13.4 %all-gather = f32[8,1,576]{2,1,0:T(1,128)S(1)} all-gather(f32[1,1,576]{2,1,0:T(1,128)S(1)} %bitcast.151), channel_id=1, replica_groups=mesh['row'=8,'col'=8,'track'=4] {'row'}, dimensions={0}, use_global_device_ids=true | all-gather | bytes 20736 | tf_op jit(solution)/shard_map/all_gather | solution.py:97
  769.4 0.3 convolution_bitcast_fusion.3
  769.6 0.3 convolution_bitcast_fusion.2
  769.9 0.1 convolution_bitcast_fusion.5
  770.0 5.1 fusion.32
  775.2 3.3 fusion.16
  778.5 0.3 fusion.48
  778.7 5.1 fusion.38
  783.9 3.4 fusion.7
  787.2 0.3 convolution_add_fusion.1
  787.5 0.0 reduce-scatter.2.cloned.1.call-done
  787.6 1.4 convolution_add_fusion.4
  789.0 0.2 add.92
  789.2 1.3 convolution_reduce_fusion.1
  790.6 0.1 multiply_add_fusion.1
  790.7 73.0 %psum.51 = f32[8,576]{1,0:T(8,128)S(1)} all-reduce(f32[8,576]{1,0:T(8,128)S(1)} %multiply_add_fusion.1), channel_id=1, replica_groups=mesh['row'=8,'col'=8,'track'=4] {'row','col','track'}, use_global_device_ids=true, to_apply=%region_10.11 | all-reduce | flops 4608 | bytes 36864 | tf_op jit(solution)/shard_map/psum | solution.py:117
  863.6 0.6 multiply_reduce_fusion.2
  864.3 13.1 %all-reduce = (f32[]{:T(128)}, f32[]{:T(128)}) all-reduce(f32[]{:T(128)} %get-tuple-element.6, f32[]{:T(128)} %get-tuple-element.5), channel_id=1, replica_groups=mesh['row'=8,'col'=8,'track'=4] {'row'}, use_global_device_ids=true, to_apply=%region_4.5 | all-reduce | flops 2 | bytes 16 | tf_op jit(solution)/shard_map/psum | solution.py:11
  878.7 0.6 multiply_reduce_fusion.1
  879.3 15.3 %psum.53 = f32[]{:T(128)} all-reduce(f32[]{:T(128)} %get-tuple-element.9), channel_id=1, replica_groups=mesh['row'=8,'col'=8,'track'=4] {'row'}, use_global_device_ids=true, to_apply=%region_14.15 | all-reduce | flops 1 | bytes 8 | tf_op jit(solution)/shard_map/psum | solution.py:11
  895.9 13.4 %all-gather.1 = f32[8,1,576]{2,1,0:T(1,128)S(1)} all-gather(f32[1,1,576]{2,1,0:T(1,128)S(1)} %bitcast.152), channel_id=1, replica_groups=mesh['row'=8,'col'=8,'track'=4] {'row'}, dimensions={0}, use_global_device_ids=true | all-gather | bytes 20736 | tf_op jit(solution)/shard_map/all_gather | solution.py:97
  909.3 0.3 convolution_bitcast_fusion.1
  909.6 0.3 convolution_bitcast_fusion
  909.9 0.1 convolution_bitcast_fusion.4
  910.0 5.3 fusion.35
  915.3 3.3 fusion.12
  918.6 0.3 fusion.45
  918.9 5.1 fusion.41
  924.0 1.5 fusion.3
  925.6 0.3 convolution_add_fusion
  925.9 0.4 convolution_add_fusion.3
  926.3 0.2 add.98
  926.5 0.4 convolution_reduce_fusion
  926.9 0.1 multiply_add_fusion
  927.0 73.7 %psum.54 = f32[8,576]{1,0:T(8,128)S(1)} all-reduce(f32[8,576]{1,0:T(8,128)S(1)} %multiply_add_fusion), channel_id=1, replica_groups=mesh['row'=8,'col'=8,'track'=4] {'row','col','track'}, use_global_device_ids=true, to_apply=%region_15.16 | all-reduce | flops 4608 | bytes 36864 | tf_op jit(solution)/shard_map/psum | solution.py:117
  1000.7 0.6 multiply_reduce_fusion
  1001.3 13.1 %psum.55 = f32[]{:T(128)} all-reduce(f32[]{:T(128)} %multiply_reduce_fusion), channel_id=1, replica_groups=mesh['row'=8,'col'=8,'track'=4] {'row'}, use_global_device_ids=true, to_apply=%region_17.18 | all-reduce | flops 1 | bytes 8 | tf_op jit(solution)/shard_map/psum | solution.py:122
  1015.7 0.6 subtract_divide_fusion
  (18 shorter events, 0.1 us)
Async XLA Ops:
  9.8 41.2 %all-to-all-start.1 = ((s32[64,1,3]{2,1,0:T(1,128)}), s32[64,1,3]{2,1,0:T(1,128)S(1)}, u32[]{:S(2)}, u32[]{:S(2)}) async-start(s32[64,1,3]{2,1,0:T(1,128)} %bitcast.21), calls=%async_computation.1 | async-start | bytes 65536 | tf_op jit(solution)/shard_map/all_to_all | solution.py:64
  51.0 10.8 %copy-start.3 = (s32[64,2]{0,1:T(2,128)S(1)}, s32[64,2]{0,1:T(2,128)}, u32[]{:S(2)}) copy-start(s32[64,2]{0,1:T(2,128)} %param.6) | copy-start | bytes 1540
  51.1 359.4 %all-to-all-start = ((f32[64,3,2,16,576]{4,3,2,1,0:T(8,128)}), f32[64,3,2,16,576]{4,3,2,1,0:T(8,128)}, u32[]{:S(2)}, u32[]{:S(2)}) async-start(f32[64,3,2,16,576]{4,3,2,1,0:T(8,128)} %bitcast.149), calls=%async_computation | async-start | bytes 31457280 | tf_op jit(solution)/shard_map/all_to_all | solution.py:57
  61.8 725.8 %reduce-scatter.2.cloned.1.call-start = ((), (), s32[]{:S(2)}) async-start(), calls=%async_computation.3 | async-start | bytes 1843200 | tf_op jit(solution)/shard_map/reduce_scatter | solution.py:87
  418.1 337.9 %copy-start.1 = (f32[1,576]{1,0:T(1,128)S(1)}, f32[1,576]{1,0:T(1,128)}, u32[]{:S(2)}) copy-start(f32[1,576]{1,0:T(1,128)} %param.8) | copy-start | bytes 6916
  418.1 337.8 %copy-start.2 = (f32[1,576]{1,0:T(1,128)S(1)}, f32[1,576]{1,0:T(1,128)}, u32[]{:S(2)}) copy-start(f32[1,576]{1,0:T(1,128)} %param.9) | copy-start | bytes 6916
  783.9 140.1 %slice-start = ((s8[5242880]{0:T(1024)(128)(4,1)}), s8[1048576]{0:T(1024)(128)(4,1)S(1)}, s32[]{:S(2)}) async-start(s8[5242880]{0:T(1024)(128)(4,1)} %bitcast.147), calls=%async_computation.4 | async-start | bytes 2097152
  910.0 14.0 %slice-start.1 = ((s8[5242880]{0:T(1024)(128)(4,1)}), s8[4194304]{0:T(1024)(128)(4,1)S(1)}, s32[]{:S(2)}) async-start(s8[5242880]{0:T(1024)(128)(4,1)} %bitcast.147), calls=%async_computation.5 | async-start | bytes 8388608
  910.0 15.8 %copy-start = (f32[144,576]{1,0:T(8,128)S(1)}, f32[144,576]{1,0:T(8,128)}, u32[]{:S(2)}) copy-start(f32[144,576]{1,0:T(8,128)} %reduce-scatter.2.cloned.1.call-done) | copy-start | bytes 995332
Sparse Core Ops, SparseCore 0:
  665.8 38.9 reduce-scatter.1
where the time goes:
time: 1020 us
  waiting for transfers between devices  345 us (34%)
  blocking collectives  305 us (30%)
  matrix products  286 us (28%)
  local copies, waits for them, and re-layouts  26.5 us (3%)
  starting transfers between devices  23.9 us (2%)
  other arithmetic  18.8 us (2%)
  between operations  18.3 us (2%)
    all_to_all x1, waiting for transfers between devices, on_device(): lax.all_to_all(outgoing.reshape(owners, capacity, 2, jac_rows, params), (...  345 us
    dot_general x1, matrix products, on_device(): jnp.einsum('mkr,mkc->rc', received_rows * slot_mask[:, None, None], recei...  248 us
    psum x2, blocking collectives, on_device(): summed = lax.psum(local, ('row', 'col', 'track'))  147 us
    psum x1, blocking collectives, on_device(): diag_all = lax.psum(diag_part, ('row', 'col', 'track'))  89.9 us
    psum x2, blocking collectives, fitness_sum(): return lax.psum(jnp.sum(residual * scaled), 'row')  28.3 us
    all_gather x2, blocking collectives, on_device(): full_dir = lax.all_gather(direction, 'row', axis=0, tiled=True)  26.8 us
  transfers between devices with their start and end apart: 3, of which 1 were waited for; matrix products, arithmetic and copies ran while one was open for 5% of the time, Pallas kernels for 0%

commit v1 on v0

--- a/solution.py
+++ b/solution.py
@@ -37,7 +37,7 @@
     diag_part = diag_part + jnp.dot(
         high_onehot.T, jnp.sum(high_side * high_side, axis=1), precision=highest
     )
-    diag_all = lax.psum(diag_part, ("row", "col", "track"))
+    diag_all = jnp.sum(lax.all_gather(diag_part, ("row", "col", "track")), axis=0)
     precond = damping + lax.dynamic_slice_in_dim(diag_all, row_id * row_clusters, row_clusters, 0)
     flipped = filed_flip == 1
     filed_row = jnp.where(flipped, high_cluster, low_cluster)

time: 1020 us -> 964 us (0.945)
  blocking collectives: 305 us -> 230 us
  waiting for transfers between devices: 345 us -> 356 us
    psum x1 -> x0, blocking collectives: 89.9 us -> none  [on_device(): diag_all = lax.psum(diag_part, ('row', 'col', 'track'))]
  transfers between devices with their start and end apart: 3 -> 4, of which waited for: 1 -> 2; matrix products, arithmetic and copies ran while one was open for 5% -> 32% of each run, Pallas kernels for 0% -> 0%
where the time goes in v1:
time: 964 us; the launch traced here: 963 us
  waiting for transfers between devices  356 us (37%)
  matrix products  285 us (30%)
  blocking collectives  230 us (24%)
  local copies, waits for them, and re-layouts  26.6 us (3%)
  starting transfers between devices  23.7 us (2%)
  other arithmetic  21.8 us (2%)
  between operations  19.8 us (2%)
    all_to_all x1, waiting for transfers between devices, on_device(): lax.all_to_all(outgoing.reshape(owners, capacity, 2, jac_rows, params), (...  352 us
    dot_general x1, matrix products, on_device(): jnp.einsum('mkr,mkc->rc', received_rows * slot_mask[:, None, None], recei...  248 us
    psum x2, blocking collectives, on_device(): summed = lax.psum(local, ('row', 'col', 'track'))  157 us
    all_gather x2, blocking collectives, on_device(): full_dir = lax.all_gather(direction, 'row', axis=0, tiled=True)  33.1 us
    psum x2, blocking collectives, fitness_sum(): return lax.psum(jnp.sum(residual * scaled), 'row')  27.5 us
  transfers between devices with their start and end apart: 4, of which 2 were waited for; matrix products, arithmetic and copies ran while one was open for 32% of the time, Pallas kernels for 0%

profile of v1, /device:TPU:1, one launch (start us, length us, event | category | flops | bytes accessed | tf_op | source)
XLA Modules:
  0.0 963.3 jit_solution(15248693931741420003)
XLA Ops:
  8.0 0.8 select_add_fusion
  8.8 0.1 fusion.59
  8.8 0.1 reduce_window_sum.11
  8.9 0.2 select_reduce_fusion
  9.1 0.8 scatter_custom_fusion.1
  9.9 0.8 all_to_all.10
  10.7 13.1 %all-to-all-start.1 = ((s32[64,1,3]{2,1,0:T(1,128)}), s32[64,1,3]{2,1,0:T(1,128)S(1)}, u32[]{:S(2)}, u32[]{:S(2)}) async-start(s32[64,1,3]{2,1,0:T(1,128)} %bitcast.22), calls=%async_computation.1 | async-start | bytes 65536 | tf_op jit(solution)/shard_map/all_to_all | solution.py:64
  23.8 0.7 broadcast_compare_fusion
  24.5 6.9 reverse_select_fusion
  31.4 7.5 broadcast_in_dim.12
  38.9 13.2 %scatter_fusion = f32[192,2,16,576]{3,2,1,0:T(8,128)} fusion(f32[192,2,16,576]{3,2,1,0:T(8,128)} %broadcast_in_dim.12, s32[64]{0:T(128)S(1)} %compare_select_fusion, f32[64,2,16,576]{3,2,1,0:T(8,128)} %reverse_select_fusion), kind=kCustom, calls=%fused_computation | custom fusion | bytes 14156032 | tf_op jit(solution)/shard_map/scatter | solution.py:53
  52.1 10.5 %all-to-all-start = ((f32[64,3,2,16,576]{4,3,2,1,0:T(8,128)}), f32[64,3,2,16,576]{4,3,2,1,0:T(8,128)}, u32[]{:S(2)}, u32[]{:S(2)}) async-start(f32[64,3,2,16,576]{4,3,2,1,0:T(8,128)} %bitcast.153), calls=%async_computation | async-start | bytes 31457280 | tf_op jit(solution)/shard_map/all_to_all | solution.py:57
  62.6 0.0 all-gather.5.cloned.1.call-start
  62.7 3.6 fusion.11
  66.2 0.3 fusion.60
  66.5 0.9 convolution_add_fusion.2
  67.4 0.0 reduce-scatter.2.cloned.1.call-start
  67.5 0.1 fusion.58
  67.6 0.1 reshape.60
  67.7 351.6 %all-to-all-done = f32[64,3,2,16,576]{4,3,2,1,0:T(8,128)} async-done(((f32[64,3,2,16,576]{4,3,2,1,0:T(8,128)}), f32[64,3,2,16,576]{4,3,2,1,0:T(8,128)}, u32[]{:S(2)}, u32[]{:S(2)}) %all-to-all-start) | async-done | bytes 14155808 | tf_op jit(solution)/shard_map/all_to_all | solution.py:57
  419.3 3.8 slice.25
  423.1 3.8 fusion
  426.9 247.6 %fusion.29 = f32[576,576]{1,0:T(8,128)} fusion(f32[192,1,16,576]{3,2,1,0:T(8,128)S(1)} %slice.25, f32[192,16,576]{2,1,0:T(8,128)S(1)} %fusion), kind=kOutput, calls=%fused_computation.37 | convolution fusion | flops 12230590464 | bytes 15482880 | tf_op jit(solution)/shard_map/mkr,mkc->rc/dot_general | solution.py:78
  674.5 0.0 reduce-scatter.2.cloned.1.call-update
  674.6 0.0 all-gather.5.cloned.1.call-done
  674.6 2.9 bitcast_reduce_fusion
  677.6 19.6 %all-gather.1 = f32[8,1,576]{2,1,0:T(1,128)S(1)} all-gather(f32[1,1,576]{2,1,0:T(1,128)S(1)} %bitcast.155), channel_id=1, replica_groups=mesh['row'=8,'col'=8,'track'=4] {'row'}, dimensions={0}, use_global_device_ids=true | all-gather | bytes 20736 | tf_op jit(solution)/shard_map/all_gather | solution.py:97
  697.2 0.3 convolution_bitcast_fusion.3
  697.5 0.3 convolution_bitcast_fusion.2
  697.8 0.1 convolution_bitcast_fusion.5
  697.9 5.3 fusion.32
  703.2 3.3 fusion.16
  706.5 0.3 fusion.48
  706.8 5.1 fusion.38
  711.9 1.5 fusion.7
  713.5 0.3 convolution_add_fusion.1
  713.8 4.3 reduce-scatter.2.cloned.1.call-done
  718.1 1.4 convolution_add_fusion.4
  719.6 0.2 add.90
  719.8 1.3 convolution_reduce_fusion.1
  721.1 0.1 multiply_add_fusion.1
  721.2 83.8 %psum.43 = f32[8,576]{1,0:T(8,128)S(1)} all-reduce(f32[8,576]{1,0:T(8,128)S(1)} %multiply_add_fusion.1), channel_id=1, replica_groups=mesh['row'=8,'col'=8,'track'=4] {'row','col','track'}, use_global_device_ids=true, to_apply=%region_10.11 | all-reduce | flops 4608 | bytes 36864 | tf_op jit(solution)/shard_map/psum | solution.py:117
  805.0 0.6 multiply_reduce_fusion.2
  805.6 13.1 %all-reduce = (f32[]{:T(128)}, f32[]{:T(128)}) all-reduce(f32[]{:T(128)} %get-tuple-element.6, f32[]{:T(128)} %get-tuple-element.5), channel_id=1, replica_groups=mesh['row'=8,'col'=8,'track'=4] {'row'}, use_global_device_ids=true, to_apply=%region_4.5 | all-reduce | flops 2 | bytes 16 | tf_op jit(solution)/shard_map/psum | solution.py:11
  820.0 0.6 multiply_reduce_fusion.1
  820.6 14.4 %psum.45 = f32[]{:T(128)} all-reduce(f32[]{:T(128)} %get-tuple-element.9), channel_id=1, replica_groups=mesh['row'=8,'col'=8,'track'=4] {'row'}, use_global_device_ids=true, to_apply=%region_14.15 | all-reduce | flops 1 | bytes 8 | tf_op jit(solution)/shard_map/psum | solution.py:11
  836.4 13.4 %all-gather.2 = f32[8,1,576]{2,1,0:T(1,128)S(1)} all-gather(f32[1,1,576]{2,1,0:T(1,128)S(1)} %bitcast.156), channel_id=1, replica_groups=mesh['row'=8,'col'=8,'track'=4] {'row'}, dimensions={0}, use_global_device_ids=true | all-gather | bytes 20736 | tf_op jit(solution)/shard_map/all_gather | solution.py:97
  849.8 0.3 convolution_bitcast_fusion.1
  850.1 0.3 convolution_bitcast_fusion
  850.4 0.1 convolution_bitcast_fusion.4
  850.5 5.3 fusion.35
  855.8 3.3 fusion.12
  859.1 0.3 fusion.45
  859.4 5.1 fusion.41
  864.5 1.5 fusion.3
  866.1 0.3 convolution_add_fusion
  866.4 0.4 convolution_add_fusion.3
  866.8 0.2 add.96
  867.0 0.4 convolution_reduce_fusion
  867.4 0.1 multiply_add_fusion
  867.5 72.8 %psum.46 = f32[8,576]{1,0:T(8,128)S(1)} all-reduce(f32[8,576]{1,0:T(8,128)S(1)} %multiply_add_fusion), channel_id=1, replica_groups=mesh['row'=8,'col'=8,'track'=4] {'row','col','track'}, use_global_device_ids=true, to_apply=%region_15.16 | all-reduce | flops 4608 | bytes 36864 | tf_op jit(solution)/shard_map/psum | solution.py:117
  940.3 0.6 multiply_reduce_fusion
  940.9 13.1 %psum.47 = f32[]{:T(128)} all-reduce(f32[]{:T(128)} %multiply_reduce_fusion), channel_id=1, replica_groups=mesh['row'=8,'col'=8,'track'=4] {'row'}, use_global_device_ids=true, to_apply=%region_17.18 | all-reduce | flops 1 | bytes 8 | tf_op jit(solution)/shard_map/psum | solution.py:122
  955.3 0.6 subtract_divide_fusion
  (26 shorter events, 0.1 us)
Async XLA Ops:
  10.7 41.4 %all-to-all-start.1 = ((s32[64,1,3]{2,1,0:T(1,128)}), s32[64,1,3]{2,1,0:T(1,128)S(1)}, u32[]{:S(2)}, u32[]{:S(2)}) async-start(s32[64,1,3]{2,1,0:T(1,128)} %bitcast.22), calls=%async_computation.1 | async-start | bytes 65536 | tf_op jit(solution)/shard_map/all_to_all | solution.py:64
  52.1 10.5 %copy-start.3 = (s32[64,2]{0,1:T(2,128)S(1)}, s32[64,2]{0,1:T(2,128)}, u32[]{:S(2)}) copy-start(s32[64,2]{0,1:T(2,128)} %param.6) | copy-start | bytes 1540
  52.1 367.2 %all-to-all-start = ((f32[64,3,2,16,576]{4,3,2,1,0:T(8,128)}), f32[64,3,2,16,576]{4,3,2,1,0:T(8,128)}, u32[]{:S(2)}, u32[]{:S(2)}) async-start(f32[64,3,2,16,576]{4,3,2,1,0:T(8,128)} %bitcast.153), calls=%async_computation | async-start | bytes 31457280 | tf_op jit(solution)/shard_map/all_to_all | solution.py:57
  62.6 612.0 %all-gather.5.cloned.1.call-start = ((), (), s32[]{:S(2)}) async-start(), calls=%async_computation.4 | async-start | bytes 5263360 | tf_op jit(solution)/shard_map/all_gather | solution.py:40
  67.4 650.7 %reduce-scatter.2.cloned.1.call-start = ((), (), s32[]{:S(2)}) async-start(), calls=%async_computation.3 | async-start | bytes 1843200 | tf_op jit(solution)/shard_map/reduce_scatter | solution.py:87
  674.5 3.0 copy-start.1
  674.5 3.0 copy-start.2
  674.6 37.3 %slice-start = ((s8[5242880]{0:T(1024)(128)(4,1)}), s8[1048576]{0:T(1024)(128)(4,1)S(1)}, s32[]{:S(2)}) async-start(s8[5242880]{0:T(1024)(128)(4,1)} %bitcast.149), calls=%async_computation.5 | async-start | bytes 2097152
  697.9 14.0 %slice-start.1 = ((s8[5242880]{0:T(1024)(128)(4,1)}), s8[4194304]{0:T(1024)(128)(4,1)S(1)}, s32[]{:S(2)}) async-start(s8[5242880]{0:T(1024)(128)(4,1)} %bitcast.149), calls=%async_computation.6 | async-start | bytes 8388608
  711.9 152.6 %slice-start.2 = ((s8[5242880]{0:T(1024)(128)(4,1)}), s8[1048576]{0:T(1024)(128)(4,1)S(1)}, s32[]{:S(2)}) async-start(s8[5242880]{0:T(1024)(128)(4,1)} %bitcast.151), calls=%async_computation.7 | async-start | bytes 2097152
  850.5 14.0 %slice-start.3 = ((s8[5242880]{0:T(1024)(128)(4,1)}), s8[4194304]{0:T(1024)(128)(4,1)S(1)}, s32[]{:S(2)}) async-start(s8[5242880]{0:T(1024)(128)(4,1)} %bitcast.151), calls=%async_computation.8 | async-start | bytes 8388608
  850.5 15.8 %copy-start = (f32[144,576]{1,0:T(8,128)S(1)}, f32[144,576]{1,0:T(8,128)}, u32[]{:S(2)}) copy-start(f32[144,576]{1,0:T(8,128)} %reduce-scatter.2.cloned.1.call-done) | copy-start | bytes 995332
Sparse Core Ops, SparseCore 0:
  67.6 222.2 all-gather.4
Sparse Core Ops, SparseCore 1:
  674.6 43.4 reduce-scatter.1
